TPU v7x, 512 devices: a whole 4x4x16 slice. The times are simulated.
512 devices in a mesh: blk: 32 (over z, core), ctr: 16 (over x, y).
Axes of the slice: x: 4, y: 4, z: 16, core: 2. Of those that a mesh axis runs over, the one named last changes fastest.
Arguments:
- integrals: float32 [32, 800, 12800], P('blk', None, 'ctr'), may hold values from -0.078125 to 0.078125
- amplitudes: float32 [8, 12800, 128], P(None, 'ctr', 'blk'), may hold values from -6 to 6
- blockmap: int32 [32], replicated, may hold values from 0 to 31, each once
- vir_energy: float32 [320], replicated, may hold values from 0.2 to 3
- occ_energy: float32 [32], replicated, may hold values from -2 to -0.3
Outputs:
- ladder: float32 [32, 800, 128], P('blk', 'ctr')
- increment: float32 [32, 800, 128], P('blk', 'ctr')
Inputs may be any that keep to these rules, and one draw needn't show every extreme that they name: `blockmap`: every block number appears in exactly one slot.
All inputs are finite; a program needn't handle non-finite values.
Results may differ from a plain program's by a relative error of at most 0.0003.
Values sent between devices are 32-bit elements; how exact they have to be, the bound alone decides.
A program may use at most 64 MiB of HBM per device.

v0:
```python
import jax
import jax.numpy as jnp
from jax import lax
from jax.sharding import PartitionSpec as P

NIRR = 8
VI = 40
OI = 4


def denominator(block, groups, ab_block, start, count, columns, vir_energy, occ_energy):
    irrep = block // groups
    rows = block % groups * ab_block + start + jnp.arange(count, dtype=jnp.int32)
    arow = rows // (VI * VI)
    first = arow * VI + rows // VI % VI
    second = jnp.bitwise_xor(arow, irrep) * VI + rows % VI
    cols = jnp.arange(columns, dtype=jnp.int32)
    orow = cols // (OI * OI)
    hole_one = orow * OI + cols // OI % OI
    hole_two = jnp.bitwise_xor(orow, irrep) * OI + cols % OI
    upper = jnp.take(vir_energy, first) + jnp.take(vir_energy, second)
    lower = jnp.take(occ_energy, hole_one) + jnp.take(occ_energy, hole_two)
    return upper[:, None] - lower[None, :]


def on_device(integrals, amplitudes, blockmap, vir_energy, occ_energy):
    blocks = lax.axis_size("blk")
    groups = blocks // NIRR
    block = blockmap[lax.axis_index("blk")]
    irrep = block // groups
    local = integrals[0]
    ab_block = local.shape[0]
    share = ab_block // lax.axis_size("ctr")
    chosen = lax.dynamic_index_in_dim(
        lax.all_gather(amplitudes, "blk", axis=2, tiled=True), irrep, 0, keepdims=False
    )
    partial_value = jnp.dot(
        local, chosen, preferred_element_type=jnp.float32, precision=lax.Precision.HIGHEST
    )
    offset = lax.axis_index("ctr") * share
    summed = lax.psum(partial_value, "ctr")
    mine = lax.dynamic_slice_in_dim(summed, offset, share, 0)
    denom = denominator(
        block, groups, ab_block, offset, share, partial_value.shape[1], vir_energy, occ_energy
    )
    return (mine[None], (mine / denom)[None])


def solution(mesh):
    placed = (P("blk", None, "ctr"), P(None, "ctr", "blk"), P(), P(), P())
    return jax.shard_map(
        on_device,
        mesh=mesh,
        in_specs=placed,
        out_specs=(P("blk", "ctr", None), P("blk", "ctr", None)),
        check_vma=False,
    )
```

profile of v0, /device:TPU:32, one launch (start us, length us, event | category | flops | bytes accessed | tf_op | source)
XLA Modules:
  0.0 216.9 jit_solution(8008306709315105640)
XLA Ops:
  7.2 0.0 copy-start
  7.2 0.0 all-gather.2.cloned.1.call-start
  7.2 1.7 copy.11
  8.9 0.0 all-gather.2.cloned.1.call-update
  9.0 0.0 all-reduce.2.cloned.1.call-start
  9.0 1.2 dynamic_slice.10
  12.9 1.5 gather_fusion
  14.4 1.5 gather_fusion.1
  15.9 1.6 gather_fusion.3
  17.5 1.6 gather_fusion.2
  19.1 68.6 %all-gather.2.cloned.1.call-done = f32[8,800,128]{1,0,2:T(8,128)} async-done(((f32[8,800,4]{1,0,2:T(8,128)}), f32[8,800,128]{1,0,2:T(8,128)}) %all-gather.2.cloned.1.call-update) | async-done | bytes 3276816 | tf_op jit(solution)/shard_map/all_gather | solution.py:35
  87.7 2.4 %constant_dynamic-slice_fusion.1 = f32[1,800,128]{1,0,2:T(1,128)S(1)} fusion(f32[8,800,128]{1,0,2:T(8,128)} %all-gather.2.cloned.1.call-done, s32[]{:T(128)S(6)} %select_n.74), kind=kLoop, calls=%fused_computation.47 | loop fusion | bytes 819204 | tf_op jit(solution)/shard_map/jit(dynamic_index_in_dim)/dynamic_slice | solution.py:34
  90.1 1.1 copy.14
  91.2 0.0 copy-done
  91.2 4.2 %fusion.2 = f32[800,128]{1,0:T(8,128)} fusion(f32[1,800,800]{2,1,0:T(8,128)S(1)} %copy-done, f32[1,800,128]{2,1,0:T(8,128)} %copy.14), kind=kOutput, calls=%fused_computation.6 | convolution fusion | flops 983040000 | bytes 3379200 | tf_op jit(solution)/shard_map/dot_general | solution.py:37
  95.4 0.0 all-reduce.2.cloned.1.call-update
  95.5 112.5 %all-reduce.2.cloned.1.call-done = f32[800,128]{1,0:T(8,128)} async-done(((f32[800,128]{1,0:T(8,128)}), f32[800,128]{1,0:T(8,128)}) %all-reduce.2.cloned.1.call-update) | async-done | bytes 409616 | tf_op jit(solution)/shard_map/psum | solution.py:41
  208.0 0.8 divide_bitcast_fusion
  208.8 0.6 copy.13
  209.5 0.6 broadcast_in_dim.20
  (9 shorter events, 0.1 us)
Async XLA Ops:
  7.2 84.0 %copy-start = (f32[1,800,800]{2,1,0:T(8,128)S(1)}, f32[1,800,800]{2,1,0:T(8,128)}, u32[]{:S(2)}) copy-start(f32[1,800,800]{2,1,0:T(8,128)} %param.9) | copy-start | bytes 7680004
  7.2 80.5 %all-gather.2.cloned.1.call-start = ((), (), s32[]{:S(2)}) async-start(), calls=%async_computation | async-start | bytes 3784704 | tf_op jit(solution)/shard_map/all_gather | solution.py:35
  9.0 199.0 %all-reduce.2.cloned.1.call-start = ((), (), s32[]{:S(2)}) async-start(), calls=%async_computation.1 | async-start | bytes 819200 | tf_op jit(solution)/shard_map/psum | solution.py:41
Sparse Core Ops, SparseCore 0:
  10.1 77.5 all-gather.1
  95.5 112.4 all-reduce.1
where the time goes:
time: 217 us
  waiting for transfers between devices  181 us (83%)
  between operations  16.7 us (8%)
  local copies, waits for them, and re-layouts  13.8 us (6%)
  matrix products  4.2 us (2%)
    psum x1, waiting for transfers between devices, on_device(): summed = lax.psum(partial_value, 'ctr')  113 us
    all_gather x1, waiting for transfers between devices, on_device(): lax.all_gather(amplitudes, 'blk', axis=2, tiled=True)  68.6 us
  transfers between devices with their start and end apart: 2, of which 2 were waited for; matrix products, arithmetic and copies ran while one was open for 3% of the time, Pallas kernels for 0%

commit v1 on v0

--- a/solution.py
+++ b/solution.py
@@ -24,6 +24,18 @@
 
 
 def on_device(integrals, amplitudes, blockmap, vir_energy, occ_energy):
+
+    def process_islands_on_mesh(in_array, d_out):
+        return jnp.concatenate(
+            lax.all_to_all(
+                jnp.stack(lax.axis_size("blk") * [in_array], axis=0),
+                axis_name="blk",
+                split_axis=0,
+                concat_axis=0,
+            ),
+            d_out,
+        )
+
     blocks = lax.axis_size("blk")
     groups = blocks // NIRR
     block = blockmap[lax.axis_index("blk")]
@@ -32,7 +44,7 @@
     ab_block = local.shape[0]
     share = ab_block // lax.axis_size("ctr")
     chosen = lax.dynamic_index_in_dim(
-        lax.all_gather(amplitudes, "blk", axis=2, tiled=True), irrep, 0, keepdims=False
+        process_islands_on_mesh(amplitudes, 2), irrep, 0, keepdims=False
     )
     partial_value = jnp.dot(
         local, chosen, preferred_element_type=jnp.float32, precision=lax.Precision.HIGHEST

time: 217 us -> 318 us (1.47)
  waiting for transfers between devices: 181 us -> 268 us
  starting transfers between devices: 0.08 us -> 15.6 us
    all_to_all x0 -> x1, waiting for transfers between devices: none -> 160 us  [process_islands_on_mesh(): lax.all_to_all(jnp.stack(lax.axis_size('blk') * [in_array], axis=0), axis...]
    all_gather x1 -> x0, waiting for transfers between devices: 68.6 us -> none  [on_device(): lax.all_gather(amplitudes, 'blk', axis=2, tiled=True)]
    all_to_all x0 -> x1, starting transfers between devices: none -> 15.5 us  [process_islands_on_mesh(): lax.all_to_all(jnp.stack(lax.axis_size('blk') * [in_array], axis=0), axis...]
    psum x1, waiting for transfers between devices: 113 us -> 108 us  [on_device(): summed = lax.psum(partial_value, 'ctr')]
  transfers between devices with their start and end apart: 2 -> 2, of which waited for: 2 -> 2; matrix products, arithmetic and copies ran while one was open for 3% -> 1% of each run, Pallas kernels for 0% -> 0%
where the time goes in v1:
time: 318 us
  waiting for transfers between devices  268 us (84%)
  between operations  16.8 us (5%)
  starting transfers between devices  15.6 us (5%)
  local copies, waits for them, and re-layouts  12.7 us (4%)
  matrix products  4.18 us (1%)
    all_to_all x1, waiting for transfers between devices, process_islands_on_mesh(): lax.all_to_all(jnp.stack(lax.axis_size('blk') * [in_array], axis=0), axis...  160 us
    psum x1, waiting for transfers between devices, on_device(): summed = lax.psum(partial_value, 'ctr')  108 us
    all_to_all x1, starting transfers between devices, process_islands_on_mesh(): lax.all_to_all(jnp.stack(lax.axis_size('blk') * [in_array], axis=0), axis...  15.5 us
  transfers between devices with their start and end apart: 2, of which 2 were waited for; matrix products, arithmetic and copies ran while one was open for 1% of the time, Pallas kernels for 0%

profile of v1, /device:TPU:32, one launch (start us, length us, event | category | flops | bytes accessed | tf_op | source)
XLA Modules:
  0.0 317.9 jit_solution(12202469258042509234)
XLA Ops:
  7.2 0.0 copy-start
  7.2 1.1 copy.11
  8.2 2.3 stack.2
  10.5 0.0 copy-start.3
  10.5 0.0 copy-start.2
  10.5 0.0 copy-start.1
  10.5 15.5 %all-to-all-start = ((f32[32,8,800,4]{2,1,3,0:T(8,128)}), f32[32,8,800,4]{2,1,3,0:T(8,128)}, u32[]{:S(2)}, u32[]{:S(2)}) async-start(f32[32,8,800,4]{2,1,3,0:T(8,128)} %stack.2), calls=%async_computation | async-start | bytes 7340032 | tf_op jit(solution)/shard_map/all_to_all | solution.py:30
  26.0 0.0 all-reduce.2.cloned.1.call-start
  26.1 0.0 copy-done.3
  26.1 0.6 dynamic_slice.10
  29.4 0.0 copy-done.2
  29.4 0.8 gather_fusion
  30.2 0.8 gather_fusion.1
  31.0 0.0 copy-done.1
  31.0 1.2 gather_fusion.3
  32.3 1.2 gather_fusion.2
  33.5 159.9 %all-to-all-done = f32[32,8,800,4]{2,1,3,0:T(8,128)} async-done(((f32[32,8,800,4]{2,1,3,0:T(8,128)}), f32[32,8,800,4]{2,1,3,0:T(8,128)}, u32[]{:S(2)}, u32[]{:S(2)}) %all-to-all-start) | async-done | bytes 3276832 | tf_op jit(solution)/shard_map/all_to_all | solution.py:30
  193.4 2.4 constant_dynamic-slice_fusion.1
  195.7 1.1 copy.12
  196.8 0.0 copy-done
  196.8 4.2 %fusion.2 = f32[800,128]{1,0:T(8,128)} fusion(f32[1,800,800]{2,1,0:T(8,128)S(1)} %copy-done, f32[1,800,128]{2,1,0:T(8,128)} %copy.12), kind=kOutput, calls=%fused_computation.6 | convolution fusion | flops 983040000 | bytes 3379200 | tf_op jit(solution)/shard_map/dot_general | solution.py:49
  201.0 0.0 all-reduce.2.cloned.1.call-update
  201.1 107.9 %all-reduce.2.cloned.1.call-done = f32[800,128]{1,0:T(8,128)} async-done(((f32[800,128]{1,0:T(8,128)}), f32[800,128]{1,0:T(8,128)}) %all-reduce.2.cloned.1.call-update) | async-done | bytes 409616 | tf_op jit(solution)/shard_map/psum | solution.py:53
  309.0 0.8 divide_bitcast_fusion
  309.8 0.6 copy.13
  310.5 0.6 broadcast_in_dim.20
  (9 shorter events, 0.1 us)
Async XLA Ops:
  7.2 189.7 %copy-start = (f32[1,800,800]{2,1,0:T(8,128)S(1)}, f32[1,800,800]{2,1,0:T(8,128)}, u32[]{:S(2)}) copy-start(f32[1,800,800]{2,1,0:T(8,128)} %param.9) | copy-start | bytes 7680004
  10.5 15.6 %copy-start.3 = (s32[32]{0:T(128)S(1)}, s32[32]{0:T(128)}, u32[]{:S(2)}) copy-start(s32[32]{0:T(128)} %param.11) | copy-start | bytes 388
  10.5 18.9 %copy-start.2 = (f32[320]{0:T(512)S(1)}, f32[320]{0:T(512)}, u32[]{:S(2)}) copy-start(f32[320]{0:T(512)} %param.12) | copy-start | bytes 3844
  10.5 20.5 %copy-start.1 = (f32[32]{0:T(128)S(1)}, f32[32]{0:T(128)}, u32[]{:S(2)}) copy-start(f32[32]{0:T(128)} %param.13) | copy-start | bytes 388
  10.5 182.9 %all-to-all-start = ((f32[32,8,800,4]{2,1,3,0:T(8,128)}), f32[32,8,800,4]{2,1,3,0:T(8,128)}, u32[]{:S(2)}, u32[]{:S(2)}) async-start(f32[32,8,800,4]{2,1,3,0:T(8,128)} %stack.2), calls=%async_computation | async-start | bytes 7340032 | tf_op jit(solution)/shard_map/all_to_all | solution.py:30
  26.0 282.9 %all-reduce.2.cloned.1.call-start = ((), (), s32[]{:S(2)}) async-start(), calls=%async_computation.1 | async-start | bytes 819200 | tf_op jit(solution)/shard_map/psum | solution.py:53
Sparse Core Ops, SparseCore 0:
  201.2 107.7 all-reduce.1

commit v2 on v0

--- a/solution.py
+++ b/solution.py
@@ -38,7 +38,8 @@
         local, chosen, preferred_element_type=jnp.float32, precision=lax.Precision.HIGHEST
     )
     offset = lax.axis_index("ctr") * share
-    summed = lax.psum(partial_value, "ctr")
+    place_types = lambda local_x: lax.all_gather(local_x, "ctr").sum(axis=0)
+    summed = place_types(partial_value)
     mine = lax.dynamic_slice_in_dim(summed, offset, share, 0)
     denom = denominator(
         block, groups, ab_block, offset, share, partial_value.shape[1], vir_energy, occ_energy

time: 217 us -> 183 us (0.84)
  the two profiles are of different devices: /device:TPU:32 before, /device:TPU:1 now
where the time goes in v2:
time: 183 us
  waiting for transfers between devices  147 us (80%)
  between operations  16.8 us (9%)
  local copies, waits for them, and re-layouts  11.7 us (6%)
  matrix products  4.21 us (2%)
  other arithmetic  3.41 us (2%)
    all_gather x1, waiting for transfers between devices, on_device(): lax.all_gather(amplitudes, 'blk', axis=2, tiled=True)  76.6 us
    all_gather x1, waiting for transfers between devices, on_device(): place_types = lambda local_x: lax.all_gather(local_x, 'ctr').sum(axis=0)  70.3 us
    dot_general x1, matrix products, on_device(): jnp.dot(local, chosen, preferred_element_type=jnp.float32, precision=lax....  4.21 us
  transfers between devices with their start and end apart: 2, of which 2 were waited for; matrix products, arithmetic and copies ran while one was open for 3% of the time, Pallas kernels for 0%

profile of v2, /device:TPU:1, one launch (start us, length us, event | category | flops | bytes accessed | tf_op | source)
XLA Modules:
  0.0 183.2 jit_solution(4115591407292680307)
XLA Ops:
  7.2 0.0 copy-start
  7.2 0.0 all-gather.4.cloned.1.call-start
  7.2 1.7 copy.8
  8.9 0.0 all-gather.4.cloned.1.call-update
  8.9 0.0 all-gather.6.cloned.1.call-start
  9.0 1.2 dynamic_slice.10
  12.9 0.0 copy-start.2
  12.9 76.6 %all-gather.4.cloned.1.call-done = f32[8,800,128]{1,0,2:T(8,128)} async-done(((f32[8,800,4]{1,0,2:T(8,128)}), f32[8,800,128]{1,0,2:T(8,128)}) %all-gather.4.cloned.1.call-update) | async-done | bytes 3276816 | tf_op jit(solution)/shard_map/all_gather | solution.py:35
  89.5 2.4 %constant_dynamic-slice_fusion.1 = f32[1,800,128]{1,0,2:T(1,128)S(1)} fusion(f32[8,800,128]{1,0,2:T(8,128)} %all-gather.4.cloned.1.call-done, s32[]{:T(128)S(6)} %select_n.74), kind=kLoop, calls=%fused_computation.47 | loop fusion | bytes 819204 | tf_op jit(solution)/shard_map/jit(dynamic_index_in_dim)/dynamic_slice | solution.py:34
  91.8 0.0 copy-start.1
  91.8 1.1 copy.10
  92.9 0.0 copy-done
  92.9 4.2 %fusion.2 = f32[800,128]{1,0:T(8,128)} fusion(f32[1,800,800]{2,1,0:T(8,128)S(1)} %copy-done, f32[1,800,128]{2,1,0:T(8,128)} %copy.10), kind=kOutput, calls=%fused_computation.6 | convolution fusion | flops 983040000 | bytes 3379200 | tf_op jit(solution)/shard_map/dot_general | solution.py:37
  97.2 0.0 all-gather.6.cloned.1.call-update
  97.2 0.0 copy-done.2
  97.2 0.8 gather_fusion
  98.1 0.8 gather_fusion.1
  98.9 0.0 copy-done.1
  98.9 1.2 gather_fusion.3
  100.1 1.2 gather_fusion.2
  101.4 70.3 %all-gather.6.cloned.1.call-done = f32[12800,128]{1,0:T(8,128)} async-done(((f32[800,128]{1,0:T(8,128)}), f32[12800,128]{1,0:T(8,128)}) %all-gather.6.cloned.1.call-update) | async-done | bytes 6553616 | tf_op jit(solution)/shard_map/all_gather | solution.py:41
  171.8 3.2 %reduce_sum.9 = f32[800,128]{1,0:T(8,128)S(1)} reduce(f32[16,800,128]{2,1,0:T(8,128)} %bitcast.12, f32[]{:T(128)} %constant.128.clone.1), dimensions={0}, to_apply=%region_0.1 | reduce | flops 1536000 | bytes 6963204 | tf_op jit(solution)/shard_map/reduce_sum | solution.py:41
  175.0 0.1 subtract_divide_fusion
  175.1 0.6 broadcast_in_dim.21
  175.7 0.6 broadcast_in_dim.20
  (9 shorter events, 0.1 us)
Async XLA Ops:
  7.2 85.8 %copy-start = (f32[1,800,800]{2,1,0:T(8,128)S(1)}, f32[1,800,800]{2,1,0:T(8,128)}, u32[]{:S(2)}) copy-start(f32[1,800,800]{2,1,0:T(8,128)} %param.9) | copy-start | bytes 7680004
  7.2 82.3 %all-gather.4.cloned.1.call-start = ((), (), s32[]{:S(2)}) async-start(), calls=%async_computation | async-start | bytes 3784704 | tf_op jit(solution)/shard_map/all_gather | solution.py:35
  8.9 162.8 %all-gather.6.cloned.1.call-start = ((), (), s32[]{:S(2)}) async-start(), calls=%async_computation.1 | async-start | bytes 6963200 | tf_op jit(solution)/shard_map/all_gather | solution.py:41
  12.9 84.4 %copy-start.2 = (f32[320]{0:T(512)S(1)}, f32[320]{0:T(512)}, u32[]{:S(2)}) copy-start(f32[320]{0:T(512)} %param.12) | copy-start | bytes 3844
  91.8 7.1 %copy-start.1 = (f32[32]{0:T(128)S(1)}, f32[32]{0:T(128)}, u32[]{:S(2)}) copy-start(f32[32]{0:T(128)} %param.13) | copy-start | bytes 388
Sparse Core Ops, SparseCore 0:
  10.1 79.2 all-gather.3
  97.3 74.4 all-gather.5
